TPU v7x, 512 devices: a whole 4x8x8 slice. The times are simulated.
512 devices in a mesh: lon: 64 (over y_lo, z, core), lat: 8 (over y_hi, x).
Axes of the slice: x: 4, y: 8 (y_hi: 2, y_lo: 4; y = y_hi * 4 + y_lo), z: 8, core: 2. Of those that a mesh axis runs over, the one named last changes fastest.
Arguments:
- final_adjoint: float32 [2, 38, 64, 8192], P(None, None, 'lat', 'lon'), may hold values from -6 to 6
- store: bfloat16 [4, 38, 16, 8, 8192], P(None, None, None, 'lat', 'lon'), may hold values from -6 to 6
- holder_offset: int32 [2, 8, 64], replicated, may hold values from 0 to 7
- holder_slot: int32 [2, 8, 64], replicated, may hold values from 0 to 15, as said below
- bottom_level: int32 [64, 8192], P('lat', 'lon'), may hold values from 0 to 38
- mix_class: int32 [37, 64, 8192], P(None, 'lat', 'lon'), may hold values from 0 to 7
- mix_table: float32 [8], replicated, may hold values from 0.02 to 0.4
Outputs:
- tracer_adjoint: float32 [2, 38, 64, 8192], P(None, None, 'lat', 'lon')
- velocity_adjoint: float32 [2, 38, 64, 8192], P(None, None, 'lat', 'lon')
Inputs may be any that keep to these rules, and one draw needn't show every extreme that they name: `holder_slot`: for every longitude tile, the 16 entries over all steps and bands are all different.
All inputs are finite; a program needn't handle non-finite values.
Results may differ from a plain program's by a relative error of at most 0.0014.
Values may be sent and summed in bfloat16 or wider, within the bound.
No kernel may reach another device: no remote copies, remote signals or barrier semaphores. Data moves between devices by JAX's collectives and lax.ppermute only.
A program may use at most 64 MiB of HBM per device.

v0:
```python
import jax
import jax.numpy as jnp
from jax import lax
from jax.sharding import PartitionSpec as P

STEPS = 2
ADVECT_HALF = 0.125
DIFFUSE = 0.1


def from_partner(block, axis, bit):
    count = lax.axis_size(axis)
    route = []
    for low in range(count):
        high = low | 1 << bit
        if high != low and high < count:
            route += [(low, high), (high, low)]
    return lax.ppermute(block, axis, route)


def with_halo(value, sides, width):
    for axis, dim in sides:
        devices, length = (lax.axis_size(axis), value.shape[dim])
        up = [(i, (i + 1) % devices) for i in range(devices)]
        down = [(j, i) for i, j in up]
        last = lax.slice_in_dim(value, length - width, length, axis=dim)
        first = lax.slice_in_dim(value, 0, width, axis=dim)
        before = lax.ppermute(last, axis, up)
        after = lax.ppermute(first, axis, down)
        value = jnp.concatenate([before, value, after], axis=dim)
    return value


def transpose_step(
    masked,
    east,
    west,
    north,
    south,
    tracer,
    tracer_east,
    tracer_north,
    zonal,
    zonal_west,
    meridional,
    meridional_south,
    south_open,
    kappa_below,
    kappa_above,
):
    below = jnp.concatenate([masked[:, 1:], jnp.zeros_like(masked[:, :1])], axis=1)
    above = jnp.concatenate([jnp.zeros_like(masked[:, :1]), masked[:, :-1]], axis=1)
    advect = (
        zonal * (east - masked)
        + zonal_west * (masked - west)
        + meridional * (north - masked)
        + meridional_south * (masked - south)
    )
    spread = east - masked + (west - masked) + (north - masked) + south_open * (south - masked)
    mixing = kappa_below * (below - masked) + kappa_above * (above - masked)
    result = masked + ADVECT_HALF * advect + DIFFUSE * spread + mixing
    zonal_grad = ADVECT_HALF * jnp.sum((tracer + tracer_east) * (east - masked), axis=0)
    merid_grad = ADVECT_HALF * jnp.sum((tracer + tracer_north) * (north - masked), axis=0)
    return (result, zonal_grad, merid_grad)


def fold_rows(row_block, field_kind):
    moved = row_block
    levels_bits = lax.axis_size("lon").bit_length() - 1
    for bit_index in range(levels_bits):
        if field_kind == "adjoint":
            moved = from_partner(moved.astype(jnp.bfloat16), "lon", bit_index).astype(moved.dtype)
        else:
            moved = from_partner(moved, "lon", bit_index)
    return jnp.flip(moved, axis=-1)


def shards(final_adjoint, store, holder_offset, holder_slot, bottom_level, mix_class, mix_table):
    band_index = lax.axis_index("lat")
    tile_index = lax.axis_index("lon")
    bands = lax.axis_size("lat")
    levels = final_adjoint.shape[1]
    tile_height = final_adjoint.shape[2]
    tile_width = final_adjoint.shape[3]
    top_band = band_index == bands - 1
    ocean_mask = (jnp.arange(levels, dtype=jnp.int32)[:, None, None] < bottom_level[None]).astype(
        jnp.float32
    )
    kappa = jnp.zeros(mix_class.shape, jnp.float32)
    for class_index in range(mix_table.shape[0]):
        kappa = kappa + mix_table[class_index] * (mix_class == class_index).astype(jnp.float32)
    zero_level = jnp.zeros((1, tile_height, tile_width), jnp.float32)
    kappa_below = jnp.concatenate([kappa, zero_level], axis=0)
    kappa_above = jnp.concatenate([zero_level, kappa], axis=0)
    global_rows = band_index * tile_height + jnp.arange(tile_height, dtype=jnp.int32)
    south_open = (global_rows > 0).astype(jnp.float32)[:, None]
    slot_table = lax.dynamic_index_in_dim(holder_slot, tile_index, axis=2, keepdims=False)
    offset_column = lax.dynamic_index_in_dim(holder_offset, tile_index, axis=2, keepdims=False)
    offset_steps = lax.dynamic_index_in_dim(offset_column, band_index, axis=1, keepdims=False)

    def sides(extended, mirrored):
        east = extended[..., 1:-1, 2:]
        west = extended[..., 1:-1, :-2]
        south = extended[..., :-2, 1:-1]
        north = extended[..., 2:, 1:-1]
        north = north.at[..., -1, :].set(jnp.where(top_band, mirrored, north[..., -1, :]))
        return (east, west, north, south)

    adjoint = final_adjoint
    zonal_total = jnp.zeros((levels, tile_height, tile_width), jnp.float32)
    merid_total = jnp.zeros((levels, tile_height, tile_width), jnp.float32)
    for step_index in range(STEPS - 1, -1, -1):
        request = jnp.take(store, slot_table[step_index], axis=2)
        received = lax.all_to_all(request, "lat", split_axis=2, concat_axis=2, tiled=True)
        order = (jnp.arange(bands, dtype=jnp.int32) + offset_steps[step_index]) % bands
        ordered = jnp.take(received, order, axis=2)
        trajectory = ordered.reshape(received.shape[0], received.shape[1], tile_height, tile_width)
        extended_state = with_halo(trajectory, (("lon", 3), ("lat", 2)), 1)
        top_state = jnp.stack([trajectory[0, :, -1], trajectory[1, :, -1], trajectory[3, :, -1]])
        mirror_state = fold_rows(top_state, "trajectory").astype(jnp.float32)
        masked = ocean_mask * adjoint
        extended_adjoint = with_halo(masked, (("lon", 3), ("lat", 2)), 1)
        mirror_adjoint = fold_rows(masked[:, :, -1, :], "adjoint")
        state_wide = extended_state.astype(jnp.float32)
        tracer = trajectory[0:2].astype(jnp.float32)
        zonal = trajectory[2].astype(jnp.float32)
        meridional = trajectory[3].astype(jnp.float32)
        tracer_east, tracer_west, tracer_north, tracer_south = sides(
            state_wide[0:2], mirror_state[0:2]
        )
        zonal_west = state_wide[2, :, 1:-1, :-2]
        meridional_south = state_wide[3, :, :-2, 1:-1] * south_open
        fold_velocity = jnp.where(top_band, mirror_state[2], 0.0)
        meridional_net = meridional.at[:, -1, :].set(meridional[:, -1, :] - fold_velocity)
        east, west, north, south = sides(extended_adjoint, mirror_adjoint)
        adjoint, zonal_grad, merid_grad = transpose_step(
            masked,
            east,
            west,
            north,
            south,
            tracer,
            tracer_east,
            tracer_north,
            zonal,
            zonal_west,
            meridional_net,
            meridional_south,
            south_open,
            kappa_below,
            kappa_above,
        )
        zonal_total = zonal_total + zonal_grad
        merid_total = merid_total + merid_grad
    return (adjoint, jnp.stack([zonal_total, merid_total]))


def solution(mesh):
    return jax.shard_map(
        shards,
        mesh=mesh,
        in_specs=(
            P(None, None, "lat", "lon"),
            P(None, None, None, "lat", "lon"),
            P(),
            P(),
            P("lat", "lon"),
            P(None, "lat", "lon"),
            P(),
        ),
        out_specs=(P(None, None, "lat", "lon"), P(None, None, "lat", "lon")),
        check_vma=False,
    )
```

profile of v0, /device:TPU:6, one launch (start us, length us, event | category | flops | bytes accessed | tf_op | source)
XLA Modules:
  0.0 261.9 jit_solution(3631502479113437797)
XLA Ops:
  4.9 10.2 %all-to-all-start = ((bf16[4,38,8,1,128]{4,0,1,3,2:T(4,128)(2,1)}), bf16[4,38,8,1,128]{4,0,1,3,2:T(4,128)(2,1)S(1)}, u32[]{:S(2)}, u32[]{:S(2)}) async-start(bf16[4,38,8,1,128]{4,0,1,3,2:T(4,128)(2,1)} %fusion.40), calls=%async_computation | async-start | bytes 622592 | tf_op jit(solution)/shard_map/all_to_all | solution.py:114
  15.9 10.2 %collective-permute-start = (f32[2,38,8,1]{3,2,1,0:T(8,128)S(1)}, f32[2,38,8,1]{3,2,1,0:T(8,128)S(1)}, u32[]{:S(2)}, u32[]{:S(2)}) collective-permute-start(f32[2,38,8,1]{3,2,1,0:T(8,128)S(1)} %get-tuple-element.132), channel_id=1, source_target_pairs={{8,0},{16,8},{24,16},{32,24},{40,32},{48,40},{56,48},{64,56},{72,6... | collective-permute-start | bytes 7304 | tf_op jit(solution)/shard_map/ppermute | solution.py:29
  35.2 5.1 %select_add_fusion = f32[37,8,128]{2,1,0:T(8,128)S(1)} fusion(s32[37,8,128]{2,1,0:T(8,128)S(1)} %copy-done.26, f32[]{:T(128)} %bitcast.28, f32[]{:T(128)} %bitcast.27, f32[]{:T(128)} %bitcast.26, f32[]{:T(128)} %bitcast.25, f32[]{:T(128)} %bitcast.24, f32[]{:T(128)} %bitcast.23, f32[]{:T(128)} %bitcast.22, f32[]{:T(128)} %bitcast.21), kind=kLoop, calls=%fused_computation.98 | loop fusion | flops 871424 | bytes 303136 | tf_op jit(solution)/shard_map/add | solution.py:91
  44.6 3.1 %collective-permute-done.14 = bf16[2,38,128]{2,0,1:T(2,128)(2,1)S(1)} collective-permute-done((bf16[2,38,128]{2,0,1:T(2,128)(2,1)S(1)}, bf16[2,38,128]{2,0,1:T(2,128)(2,1)S(1)}, u32[]{:S(2)}, u32[]{:S(2)}) %collective-permute-start.14) | collective-permute-done | bytes 19488 | tf_op jit(solution)/shard_map/ppermute | solution.py:18
  50.2 4.0 %collective-permute-done.15 = bf16[2,38,128]{2,0,1:T(2,128)(2,1)S(1)} collective-permute-done((bf16[2,38,128]{2,0,1:T(2,128)(2,1)S(1)}, bf16[2,38,128]{2,0,1:T(2,128)(2,1)S(1)}, u32[]{:S(2)}, u32[]{:S(2)}) %collective-permute-start.15) | collective-permute-done | bytes 19488 | tf_op jit(solution)/shard_map/ppermute | solution.py:18
  54.2 4.7 %collective-permute-start.16 = (bf16[2,38,128]{2,0,1:T(2,128)(2,1)S(1)}, bf16[2,38,128]{2,0,1:T(2,128)(2,1)S(1)}, u32[]{:S(2)}, u32[]{:S(2)}) collective-permute-start(bf16[2,38,128]{2,0,1:T(2,128)(2,1)S(1)} %collective-permute-done.15), channel_id=1, source_target_pairs={{0,64},{64,0},{8,72},{72,8},{16,80},{80,16},{24,88},{88,24},{32,96... | collective-permute-start | bytes 58376 | tf_op jit(solution)/shard_map/ppermute | solution.py:18
  59.5 2.8 %collective-permute-start.12 = (f32[2,38,1,130]{3,2,1,0:T(1,128)S(1)}, f32[2,38,1,130]{3,2,1,0:T(1,128)S(1)}, u32[]{:S(2)}, u32[]{:S(2)}) collective-permute-start(f32[2,38,1,130]{3,2,1,0:T(1,128)S(1)} %get-tuple-element.112), channel_id=1, source_target_pairs={{1,0},{2,1},{3,2},{4,3},{5,4},{6,5},{7,6},{0,7},{9,8},{10,9},{11,1... | collective-permute-start | bytes 118568 | tf_op jit(solution)/shard_map/ppermute | solution.py:29
  63.8 3.0 %collective-permute-start.17 = (bf16[2,38,128]{2,0,1:T(2,128)(2,1)S(1)}, bf16[2,38,128]{2,0,1:T(2,128)(2,1)S(1)}, u32[]{:S(2)}, u32[]{:S(2)}) collective-permute-start(bf16[2,38,128]{2,0,1:T(2,128)(2,1)S(1)} %collective-permute-done.16), channel_id=1, source_target_pairs={{0,128},{128,0},{8,136},{136,8},{16,144},{144,16},{24,152},{152,24... | collective-permute-start | bytes 58376 | tf_op jit(solution)/shard_map/ppermute | solution.py:18
  66.8 7.3 %collective-permute-start.19 = (f32[2,38,1,130]{3,2,1,0:T(1,128)S(1)}, f32[2,38,1,130]{3,2,1,0:T(1,128)}, u32[]{:S(2)}, u32[]{:S(2)}) collective-permute-start(f32[2,38,1,130]{3,2,1,0:T(1,128)S(1)} %get-tuple-element.113), channel_id=1, source_target_pairs={{0,1},{1,2},{2,3},{3,4},{4,5},{5,6},{6,7},{7,0},{8,9},{9,10},{10,1... | collective-permute-start | bytes 118568 | tf_op jit(solution)/shard_map/ppermute | solution.py:28
  74.1 4.4 %collective-permute-start.18 = (bf16[2,38,128]{2,0,1:T(2,128)(2,1)S(1)}, bf16[2,38,128]{2,0,1:T(2,128)(2,1)S(1)}, u32[]{:S(2)}, u32[]{:S(2)}) collective-permute-start(bf16[2,38,128]{2,0,1:T(2,128)(2,1)S(1)} %collective-permute-done.17), channel_id=1, source_target_pairs={{0,256},{256,0},{8,264},{264,8},{16,272},{272,16},{24,280},{280,24... | collective-permute-start | bytes 58376 | tf_op jit(solution)/shard_map/ppermute | solution.py:18
  81.8 9.2 %all-to-all-start.1 = ((bf16[4,38,8,1,128]{4,0,1,3,2:T(4,128)(2,1)}), bf16[4,38,8,1,128]{4,0,1,3,2:T(4,128)(2,1)S(1)}, u32[]{:S(2)}, u32[]{:S(2)}) async-start(bf16[4,38,8,1,128]{4,0,1,3,2:T(4,128)(2,1)} %fusion.39), calls=%async_computation.1 | async-start | bytes 622592 | tf_op jit(solution)/shard_map/all_to_all | solution.py:114
  93.0 8.4 %all-to-all-done.1 = bf16[4,38,8,1,128]{4,0,1,3,2:T(4,128)(2,1)S(1)} async-done(((bf16[4,38,8,1,128]{4,0,1,3,2:T(4,128)(2,1)}), bf16[4,38,8,1,128]{4,0,1,3,2:T(4,128)(2,1)S(1)}, u32[]{:S(2)}, u32[]{:S(2)}) %all-to-all-start.1) | async-done | bytes 311328 | tf_op jit(solution)/shard_map/all_to_all | solution.py:114
  105.0 7.5 %collective-permute-start.22 = (bf16[4,38,8,1]{3,2,1,0:T(8,128)(2,1)S(1)}, bf16[4,38,8,1]{3,2,1,0:T(8,128)(2,1)S(1)}, u32[]{:S(2)}, u32[]{:S(2)}) collective-permute-start(bf16[4,38,8,1]{3,2,1,0:T(8,128)(2,1)S(1)} %get-tuple-element.120), channel_id=1, source_target_pairs={{8,0},{16,8},{24,16},{32,24},{40,32},{48,40},{56,48},{64,56},{72,6... | collective-permute-start | bytes 7304 | tf_op jit(solution)/shard_map/ppermute | solution.py:29
  114.5 7.5 %collective-permute-start.2 = (bf16[4,38,8,1]{3,2,1,0:T(8,128)(2,1)}, bf16[4,38,8,1]{3,2,1,0:T(8,128)(2,1)S(1)}, u32[]{:S(2)}, u32[]{:S(2)}) collective-permute-start(bf16[4,38,8,1]{3,2,1,0:T(8,128)(2,1)} %get-tuple-element.131), channel_id=1, source_target_pairs={{8,0},{16,8},{24,16},{32,24},{40,32},{48,40},{56,48},{64,56},{72,6... | collective-permute-start | bytes 7304 | tf_op jit(solution)/shard_map/ppermute | solution.py:29
  125.6 2.4 collective-permute-start.26
  128.8 2.9 %collective-permute-start.23 = (bf16[4,38,1,130]{3,2,1,0:T(2,128)(2,1)S(1)}, bf16[4,38,1,130]{3,2,1,0:T(2,128)(2,1)S(1)}, u32[]{:S(2)}, u32[]{:S(2)}) collective-permute-start(bf16[4,38,1,130]{3,2,1,0:T(2,128)(2,1)S(1)} %get-tuple-element.106), channel_id=1, source_target_pairs={{0,1},{1,2},{2,3},{3,4},{4,5},{5,6},{6,7},{7,0},{8,9},{9,10},{10,1... | collective-permute-start | bytes 118568 | tf_op jit(solution)/shard_map/ppermute | solution.py:28
  131.7 2.9 %collective-permute-start.24 = (bf16[4,38,1,130]{3,2,1,0:T(2,128)(2,1)S(1)}, bf16[4,38,1,130]{3,2,1,0:T(2,128)(2,1)S(1)}, u32[]{:S(2)}, u32[]{:S(2)}) collective-permute-start(bf16[4,38,1,130]{3,2,1,0:T(2,128)(2,1)S(1)} %get-tuple-element.107), channel_id=1, source_target_pairs={{1,0},{2,1},{3,2},{4,3},{5,4},{6,5},{7,6},{0,7},{9,8},{10,9},{11,1... | collective-permute-start | bytes 118568 | tf_op jit(solution)/shard_map/ppermute | solution.py:29
  135.4 8.9 %collective-permute-start.3 = (bf16[4,38,1,130]{3,2,1,0:T(2,128)(2,1)S(1)}, bf16[4,38,1,130]{3,2,1,0:T(2,128)(2,1)S(1)}, u32[]{:S(2)}, u32[]{:S(2)}) collective-permute-start(bf16[4,38,1,130]{3,2,1,0:T(2,128)(2,1)S(1)} %get-tuple-element.110), channel_id=1, source_target_pairs={{0,1},{1,2},{2,3},{3,4},{4,5},{5,6},{6,7},{7,0},{8,9},{9,10},{10,1... | collective-permute-start | bytes 118568 | tf_op jit(solution)/shard_map/ppermute | solution.py:28
  148.2 3.9 %collective-permute-start.27 = (bf16[3,38,128]{2,0,1:T(4,128)(2,1)S(1)}, bf16[3,38,128]{2,0,1:T(4,128)(2,1)S(1)}, u32[]{:S(2)}, u32[]{:S(2)}) collective-permute-start(bf16[3,38,128]{2,0,1:T(4,128)(2,1)S(1)} %collective-permute-done.26), channel_id=1, source_target_pairs={{0,16},{16,0},{8,24},{24,8},{32,48},{48,32},{40,56},{56,40},{64,80... | collective-permute-start | bytes 87560 | tf_op jit(solution)/shard_map/ppermute | solution.py:18
  153.3 6.6 %collective-permute-done.4 = bf16[4,38,1,130]{3,2,1,0:T(2,128)(2,1)S(1)} collective-permute-done((bf16[4,38,1,130]{3,2,1,0:T(2,128)(2,1)S(1)}, bf16[4,38,1,130]{3,2,1,0:T(2,128)(2,1)S(1)}, u32[]{:S(2)}, u32[]{:S(2)}) %collective-permute-start.4) | collective-permute-done | bytes 39552 | tf_op jit(solution)/shard_map/ppermute | solution.py:29
  164.6 4.8 %collective-permute-start.28 = (bf16[3,38,128]{2,0,1:T(4,128)(2,1)S(1)}, bf16[3,38,128]{2,0,1:T(4,128)(2,1)S(1)}, u32[]{:S(2)}, u32[]{:S(2)}) collective-permute-start(bf16[3,38,128]{2,0,1:T(4,128)(2,1)S(1)} %collective-permute-done.27), channel_id=1, source_target_pairs={{0,32},{32,0},{8,40},{40,8},{16,48},{48,16},{24,56},{56,24},{64,96... | collective-permute-start | bytes 87560 | tf_op jit(solution)/shard_map/ppermute | solution.py:18
  172.1 7.8 %collective-permute-start.29 = (bf16[3,38,128]{2,0,1:T(4,128)(2,1)S(1)}, bf16[3,38,128]{2,0,1:T(4,128)(2,1)S(1)}, u32[]{:S(2)}, u32[]{:S(2)}) collective-permute-start(bf16[3,38,128]{2,0,1:T(4,128)(2,1)S(1)} %collective-permute-done.28), channel_id=1, source_target_pairs={{0,64},{64,0},{8,72},{72,8},{16,80},{80,16},{24,88},{88,24},{32,96... | collective-permute-start | bytes 87560 | tf_op jit(solution)/shard_map/ppermute | solution.py:18
  182.0 3.9 %collective-permute-start.30 = (bf16[3,38,128]{2,0,1:T(4,128)(2,1)S(1)}, bf16[3,38,128]{2,0,1:T(4,128)(2,1)}, u32[]{:S(2)}, u32[]{:S(2)}) collective-permute-start(bf16[3,38,128]{2,0,1:T(4,128)(2,1)S(1)} %collective-permute-done.29), channel_id=1, source_target_pairs={{0,128},{128,0},{8,136},{136,8},{16,144},{144,16},{24,152},{152,24... | collective-permute-start | bytes 87560 | tf_op jit(solution)/shard_map/ppermute | solution.py:18
  188.9 4.6 %collective-permute-start.31 = (bf16[3,38,128]{2,0,1:T(4,128)(2,1)}, bf16[3,38,128]{2,0,1:T(4,128)(2,1)}, u32[]{:S(2)}, u32[]{:S(2)}) collective-permute-start(bf16[3,38,128]{2,0,1:T(4,128)(2,1)} %collective-permute-done.30), channel_id=1, source_target_pairs={{0,256},{256,0},{8,264},{264,8},{16,272},{272,16},{24,280},{280,24... | collective-permute-start | bytes 87560 | tf_op jit(solution)/shard_map/ppermute | solution.py:18
  202.0 4.0 %collective-permute-start.20 = (f32[2,38,8,1]{3,2,1,0:T(8,128)}, f32[2,38,8,1]{3,2,1,0:T(8,128)S(1)}, u32[]{:S(2)}, u32[]{:S(2)}) collective-permute-start(f32[2,38,8,1]{3,2,1,0:T(8,128)} %get-tuple-element.121), channel_id=1, source_target_pairs={{8,0},{16,8},{24,16},{32,24},{40,32},{48,40},{56,48},{64,56},{72,6... | collective-permute-start | bytes 7304 | tf_op jit(solution)/shard_map/ppermute | solution.py:29
  210.6 3.3 %collective-permute-done.34 = bf16[2,38,128]{2,0,1:T(2,128)(2,1)} collective-permute-done((bf16[2,38,128]{2,0,1:T(2,128)(2,1)}, bf16[2,38,128]{2,0,1:T(2,128)(2,1)}, u32[]{:S(2)}, u32[]{:S(2)}) %collective-permute-start.34) | collective-permute-done | bytes 19488 | tf_op jit(solution)/shard_map/ppermute | solution.py:18
  220.8 4.3 %collective-permute-start.36 = (bf16[2,38,128]{2,0,1:T(2,128)(2,1)}, bf16[2,38,128]{2,0,1:T(2,128)(2,1)S(1)}, u32[]{:S(2)}, u32[]{:S(2)}) collective-permute-start(bf16[2,38,128]{2,0,1:T(2,128)(2,1)} %collective-permute-done.35), channel_id=1, source_target_pairs={{0,64},{64,0},{8,72},{72,8},{16,80},{80,16},{24,88},{88,24},{32,96... | collective-permute-start | bytes 58376 | tf_op jit(solution)/shard_map/ppermute | solution.py:18
  230.9 2.5 collective-permute-start.37
  239.0 9.9 %collective-permute-start.39 = (f32[2,38,1,130]{3,2,1,0:T(1,128)}, f32[2,38,1,130]{3,2,1,0:T(1,128)}, u32[]{:S(2)}, u32[]{:S(2)}) collective-permute-start(f32[2,38,1,130]{3,2,1,0:T(1,128)} %get-tuple-element.109), channel_id=1, source_target_pairs={{0,1},{1,2},{2,3},{3,4},{4,5},{5,6},{6,7},{7,0},{8,9},{9,10},{10,1... | collective-permute-start | bytes 118568 | tf_op jit(solution)/shard_map/ppermute | solution.py:28
  249.0 2.5 collective-permute-start.38
  253.0 2.8 %collective-permute-done.38 = bf16[2,38,128]{2,0,1:T(2,128)(2,1)S(1)} collective-permute-done((bf16[2,38,128]{2,0,1:T(2,128)(2,1)}, bf16[2,38,128]{2,0,1:T(2,128)(2,1)S(1)}, u32[]{:S(2)}, u32[]{:S(2)}) %collective-permute-start.38) | collective-permute-done | bytes 19488 | tf_op jit(solution)/shard_map/ppermute | solution.py:18
  259.6 2.3 fusion.15
  (205 shorter events, 92.3 us)
Async XLA Ops:
  4.9 76.3 %all-to-all-start = ((bf16[4,38,8,1,128]{4,0,1,3,2:T(4,128)(2,1)}), bf16[4,38,8,1,128]{4,0,1,3,2:T(4,128)(2,1)S(1)}, u32[]{:S(2)}, u32[]{:S(2)}) async-start(bf16[4,38,8,1,128]{4,0,1,3,2:T(4,128)(2,1)} %fusion.40), calls=%async_computation | async-start | bytes 622592 | tf_op jit(solution)/shard_map/all_to_all | solution.py:114
  15.9 43.0 %collective-permute-start = (f32[2,38,8,1]{3,2,1,0:T(8,128)S(1)}, f32[2,38,8,1]{3,2,1,0:T(8,128)S(1)}, u32[]{:S(2)}, u32[]{:S(2)}) collective-permute-start(f32[2,38,8,1]{3,2,1,0:T(8,128)S(1)} %get-tuple-element.132), channel_id=1, source_target_pairs={{8,0},{16,8},{24,16},{32,24},{40,32},{48,40},{56,48},{64,56},{72,6... | collective-permute-start | bytes 7304 | tf_op jit(solution)/shard_map/ppermute | solution.py:29
  26.1 32.9 %collective-permute-start.5 = (f32[2,38,8,1]{3,2,1,0:T(8,128)S(1)}, f32[2,38,8,1]{3,2,1,0:T(8,128)S(1)}, u32[]{:S(2)}, u32[]{:S(2)}) collective-permute-start(f32[2,38,8,1]{3,2,1,0:T(8,128)S(1)} %get-tuple-element.133), channel_id=1, source_target_pairs={{0,8},{8,16},{16,24},{24,32},{32,40},{40,48},{48,56},{56,64},{64,7... | collective-permute-start | bytes 7304 | tf_op jit(solution)/shard_map/ppermute | solution.py:28
  28.1 13.9 %collective-permute-start.13 = (bf16[2,38,128]{2,0,1:T(2,128)(2,1)S(1)}, bf16[2,38,128]{2,0,1:T(2,128)(2,1)S(1)}, u32[]{:S(2)}, u32[]{:S(2)}) collective-permute-start(bf16[2,38,128]{2,0,1:T(2,128)(2,1)S(1)} %bitcast.147), channel_id=1, source_target_pairs={{0,8},{8,0},{16,24},{24,16},{32,40},{40,32},{48,56},{56,48},{64,72... | collective-permute-start | bytes 58376 | tf_op jit(solution)/shard_map/ppermute | solution.py:18
  54.2 9.6 %collective-permute-start.16 = (bf16[2,38,128]{2,0,1:T(2,128)(2,1)S(1)}, bf16[2,38,128]{2,0,1:T(2,128)(2,1)S(1)}, u32[]{:S(2)}, u32[]{:S(2)}) collective-permute-start(bf16[2,38,128]{2,0,1:T(2,128)(2,1)S(1)} %collective-permute-done.15), channel_id=1, source_target_pairs={{0,64},{64,0},{8,72},{72,8},{16,80},{80,16},{24,88},{88,24},{32,96... | collective-permute-start | bytes 58376 | tf_op jit(solution)/shard_map/ppermute | solution.py:18
  59.5 19.0 %collective-permute-start.12 = (f32[2,38,1,130]{3,2,1,0:T(1,128)S(1)}, f32[2,38,1,130]{3,2,1,0:T(1,128)S(1)}, u32[]{:S(2)}, u32[]{:S(2)}) collective-permute-start(f32[2,38,1,130]{3,2,1,0:T(1,128)S(1)} %get-tuple-element.112), channel_id=1, source_target_pairs={{1,0},{2,1},{3,2},{4,3},{5,4},{6,5},{7,6},{0,7},{9,8},{10,9},{11,1... | collective-permute-start | bytes 118568 | tf_op jit(solution)/shard_map/ppermute | solution.py:29
  63.8 10.3 %collective-permute-start.17 = (bf16[2,38,128]{2,0,1:T(2,128)(2,1)S(1)}, bf16[2,38,128]{2,0,1:T(2,128)(2,1)S(1)}, u32[]{:S(2)}, u32[]{:S(2)}) collective-permute-start(bf16[2,38,128]{2,0,1:T(2,128)(2,1)S(1)} %collective-permute-done.16), channel_id=1, source_target_pairs={{0,128},{128,0},{8,136},{136,8},{16,144},{144,16},{24,152},{152,24... | collective-permute-start | bytes 58376 | tf_op jit(solution)/shard_map/ppermute | solution.py:18
  66.8 127.2 %collective-permute-start.19 = (f32[2,38,1,130]{3,2,1,0:T(1,128)S(1)}, f32[2,38,1,130]{3,2,1,0:T(1,128)}, u32[]{:S(2)}, u32[]{:S(2)}) collective-permute-start(f32[2,38,1,130]{3,2,1,0:T(1,128)S(1)} %get-tuple-element.113), channel_id=1, source_target_pairs={{0,1},{1,2},{2,3},{3,4},{4,5},{5,6},{6,7},{7,0},{8,9},{9,10},{10,1... | collective-permute-start | bytes 118568 | tf_op jit(solution)/shard_map/ppermute | solution.py:28
  81.8 19.6 %all-to-all-start.1 = ((bf16[4,38,8,1,128]{4,0,1,3,2:T(4,128)(2,1)}), bf16[4,38,8,1,128]{4,0,1,3,2:T(4,128)(2,1)S(1)}, u32[]{:S(2)}, u32[]{:S(2)}) async-start(bf16[4,38,8,1,128]{4,0,1,3,2:T(4,128)(2,1)} %fusion.39), calls=%async_computation.1 | async-start | bytes 622592 | tf_op jit(solution)/shard_map/all_to_all | solution.py:114
  103.0 20.6 %collective-permute-start.21 = (bf16[4,38,8,1]{3,2,1,0:T(8,128)(2,1)S(1)}, bf16[4,38,8,1]{3,2,1,0:T(8,128)(2,1)S(1)}, u32[]{:S(2)}, u32[]{:S(2)}) collective-permute-start(bf16[4,38,8,1]{3,2,1,0:T(8,128)(2,1)S(1)} %get-tuple-element.119), channel_id=1, source_target_pairs={{0,8},{8,16},{16,24},{24,32},{32,40},{40,48},{48,56},{56,64},{64,7... | collective-permute-start | bytes 7304 | tf_op jit(solution)/shard_map/ppermute | solution.py:28
  105.0 20.6 %collective-permute-start.22 = (bf16[4,38,8,1]{3,2,1,0:T(8,128)(2,1)S(1)}, bf16[4,38,8,1]{3,2,1,0:T(8,128)(2,1)S(1)}, u32[]{:S(2)}, u32[]{:S(2)}) collective-permute-start(bf16[4,38,8,1]{3,2,1,0:T(8,128)(2,1)S(1)} %get-tuple-element.120), channel_id=1, source_target_pairs={{8,0},{16,8},{24,16},{32,24},{40,32},{48,40},{56,48},{64,56},{72,6... | collective-permute-start | bytes 7304 | tf_op jit(solution)/shard_map/ppermute | solution.py:29
  112.5 16.2 %collective-permute-start.1 = (bf16[4,38,8,1]{3,2,1,0:T(8,128)(2,1)S(1)}, bf16[4,38,8,1]{3,2,1,0:T(8,128)(2,1)S(1)}, u32[]{:S(2)}, u32[]{:S(2)}) collective-permute-start(bf16[4,38,8,1]{3,2,1,0:T(8,128)(2,1)S(1)} %get-tuple-element.130), channel_id=1, source_target_pairs={{0,8},{8,16},{16,24},{24,32},{32,40},{40,48},{48,56},{56,64},{64,7... | collective-permute-start | bytes 7304 | tf_op jit(solution)/shard_map/ppermute | solution.py:28
  114.5 17.2 %collective-permute-start.2 = (bf16[4,38,8,1]{3,2,1,0:T(8,128)(2,1)}, bf16[4,38,8,1]{3,2,1,0:T(8,128)(2,1)S(1)}, u32[]{:S(2)}, u32[]{:S(2)}) collective-permute-start(bf16[4,38,8,1]{3,2,1,0:T(8,128)(2,1)} %get-tuple-element.131), channel_id=1, source_target_pairs={{8,0},{16,8},{24,16},{32,24},{40,32},{48,40},{56,48},{64,56},{72,6... | collective-permute-start | bytes 7304 | tf_op jit(solution)/shard_map/ppermute | solution.py:29
  123.6 11.8 %collective-permute-start.6 = (bf16[3,38,128]{2,0,1:T(4,128)(2,1)S(1)}, bf16[3,38,128]{2,0,1:T(4,128)(2,1)S(1)}, u32[]{:S(2)}, u32[]{:S(2)}) collective-permute-start(bf16[3,38,128]{2,0,1:T(4,128)(2,1)S(1)} %pad_maximum_fusion.37), channel_id=1, source_target_pairs={{0,8},{8,0},{16,24},{24,16},{32,40},{40,32},{48,56},{56,48},{64,72... | collective-permute-start | bytes 87560 | tf_op jit(solution)/shard_map/ppermute | solution.py:18
  125.6 18.8 %collective-permute-start.26 = (bf16[3,38,128]{2,0,1:T(4,128)(2,1)S(1)}, bf16[3,38,128]{2,0,1:T(4,128)(2,1)S(1)}, u32[]{:S(2)}, u32[]{:S(2)}) collective-permute-start(bf16[3,38,128]{2,0,1:T(4,128)(2,1)S(1)} %pad_maximum_fusion.38), channel_id=1, source_target_pairs={{0,8},{8,0},{16,24},{24,16},{32,40},{40,32},{48,56},{56,48},{64,72... | collective-permute-start | bytes 87560 | tf_op jit(solution)/shard_map/ppermute | solution.py:18
  128.8 17.5 %collective-permute-start.23 = (bf16[4,38,1,130]{3,2,1,0:T(2,128)(2,1)S(1)}, bf16[4,38,1,130]{3,2,1,0:T(2,128)(2,1)S(1)}, u32[]{:S(2)}, u32[]{:S(2)}) collective-permute-start(bf16[4,38,1,130]{3,2,1,0:T(2,128)(2,1)S(1)} %get-tuple-element.106), channel_id=1, source_target_pairs={{0,1},{1,2},{2,3},{3,4},{4,5},{5,6},{6,7},{7,0},{8,9},{9,10},{10,1... | collective-permute-start | bytes 118568 | tf_op jit(solution)/shard_map/ppermute | solution.py:28
  131.7 16.5 %collective-permute-start.24 = (bf16[4,38,1,130]{3,2,1,0:T(2,128)(2,1)S(1)}, bf16[4,38,1,130]{3,2,1,0:T(2,128)(2,1)S(1)}, u32[]{:S(2)}, u32[]{:S(2)}) collective-permute-start(bf16[4,38,1,130]{3,2,1,0:T(2,128)(2,1)S(1)} %get-tuple-element.107), channel_id=1, source_target_pairs={{1,0},{2,1},{3,2},{4,3},{5,4},{6,5},{7,6},{0,7},{9,8},{10,9},{11,1... | collective-permute-start | bytes 118568 | tf_op jit(solution)/shard_map/ppermute | solution.py:29
  135.4 17.9 %collective-permute-start.3 = (bf16[4,38,1,130]{3,2,1,0:T(2,128)(2,1)S(1)}, bf16[4,38,1,130]{3,2,1,0:T(2,128)(2,1)S(1)}, u32[]{:S(2)}, u32[]{:S(2)}) collective-permute-start(bf16[4,38,1,130]{3,2,1,0:T(2,128)(2,1)S(1)} %get-tuple-element.110), channel_id=1, source_target_pairs={{0,1},{1,2},{2,3},{3,4},{4,5},{5,6},{6,7},{7,0},{8,9},{9,10},{10,1... | collective-permute-start | bytes 118568 | tf_op jit(solution)/shard_map/ppermute | solution.py:28
  144.4 15.5 %collective-permute-start.4 = (bf16[4,38,1,130]{3,2,1,0:T(2,128)(2,1)S(1)}, bf16[4,38,1,130]{3,2,1,0:T(2,128)(2,1)S(1)}, u32[]{:S(2)}, u32[]{:S(2)}) collective-permute-start(bf16[4,38,1,130]{3,2,1,0:T(2,128)(2,1)S(1)} %get-tuple-element.111), channel_id=1, source_target_pairs={{1,0},{2,1},{3,2},{4,3},{5,4},{6,5},{7,6},{0,7},{9,8},{10,9},{11,1... | collective-permute-start | bytes 118568 | tf_op jit(solution)/shard_map/ppermute | solution.py:29
  146.3 15.6 %collective-permute-start.7 = (bf16[3,38,128]{2,0,1:T(4,128)(2,1)S(1)}, bf16[3,38,128]{2,0,1:T(4,128)(2,1)S(1)}, u32[]{:S(2)}, u32[]{:S(2)}) collective-permute-start(bf16[3,38,128]{2,0,1:T(4,128)(2,1)S(1)} %collective-permute-done.6), channel_id=1, source_target_pairs={{0,16},{16,0},{8,24},{24,8},{32,48},{48,32},{40,56},{56,40},{64,80... | collective-permute-start | bytes 87560 | tf_op jit(solution)/shard_map/ppermute | solution.py:18
  148.2 16.3 %collective-permute-start.27 = (bf16[3,38,128]{2,0,1:T(4,128)(2,1)S(1)}, bf16[3,38,128]{2,0,1:T(4,128)(2,1)S(1)}, u32[]{:S(2)}, u32[]{:S(2)}) collective-permute-start(bf16[3,38,128]{2,0,1:T(4,128)(2,1)S(1)} %collective-permute-done.26), channel_id=1, source_target_pairs={{0,16},{16,0},{8,24},{24,8},{32,48},{48,32},{40,56},{56,40},{64,80... | collective-permute-start | bytes 87560 | tf_op jit(solution)/shard_map/ppermute | solution.py:18
  169.4 10.5 %collective-permute-start.9 = (bf16[3,38,128]{2,0,1:T(4,128)(2,1)S(1)}, bf16[3,38,128]{2,0,1:T(4,128)(2,1)S(1)}, u32[]{:S(2)}, u32[]{:S(2)}) collective-permute-start(bf16[3,38,128]{2,0,1:T(4,128)(2,1)S(1)} %collective-permute-done.8), channel_id=1, source_target_pairs={{0,64},{64,0},{8,72},{72,8},{16,80},{80,16},{24,88},{88,24},{32,96... | collective-permute-start | bytes 87560 | tf_op jit(solution)/shard_map/ppermute | solution.py:18
  172.1 9.9 %collective-permute-start.29 = (bf16[3,38,128]{2,0,1:T(4,128)(2,1)S(1)}, bf16[3,38,128]{2,0,1:T(4,128)(2,1)S(1)}, u32[]{:S(2)}, u32[]{:S(2)}) collective-permute-start(bf16[3,38,128]{2,0,1:T(4,128)(2,1)S(1)} %collective-permute-done.28), channel_id=1, source_target_pairs={{0,64},{64,0},{8,72},{72,8},{16,80},{80,16},{24,88},{88,24},{32,96... | collective-permute-start | bytes 87560 | tf_op jit(solution)/shard_map/ppermute | solution.py:18
  186.0 7.5 %collective-permute-start.11 = (bf16[3,38,128]{2,0,1:T(4,128)(2,1)S(1)}, bf16[3,38,128]{2,0,1:T(4,128)(2,1)S(1)}, u32[]{:S(2)}, u32[]{:S(2)}) collective-permute-start(bf16[3,38,128]{2,0,1:T(4,128)(2,1)S(1)} %collective-permute-done.10), channel_id=1, source_target_pairs={{0,256},{256,0},{8,264},{264,8},{16,272},{272,16},{24,280},{280,24... | collective-permute-start | bytes 87560 | tf_op jit(solution)/shard_map/ppermute | solution.py:18
  188.9 12.2 %collective-permute-start.31 = (bf16[3,38,128]{2,0,1:T(4,128)(2,1)}, bf16[3,38,128]{2,0,1:T(4,128)(2,1)}, u32[]{:S(2)}, u32[]{:S(2)}) collective-permute-start(bf16[3,38,128]{2,0,1:T(4,128)(2,1)} %collective-permute-done.30), channel_id=1, source_target_pairs={{0,256},{256,0},{8,264},{264,8},{16,272},{272,16},{24,280},{280,24... | collective-permute-start | bytes 87560 | tf_op jit(solution)/shard_map/ppermute | solution.py:18
  198.3 9.7 %collective-permute-start.33 = (bf16[2,38,128]{2,0,1:T(2,128)(2,1)}, bf16[2,38,128]{2,0,1:T(2,128)(2,1)}, u32[]{:S(2)}, u32[]{:S(2)}) collective-permute-start(bf16[2,38,128]{2,0,1:T(2,128)(2,1)} %bitcast.142), channel_id=1, source_target_pairs={{0,8},{8,0},{16,24},{24,16},{32,40},{40,32},{48,56},{56,48},{64,72... | collective-permute-start | bytes 58376 | tf_op jit(solution)/shard_map/ppermute | solution.py:18
  202.0 23.0 %collective-permute-start.20 = (f32[2,38,8,1]{3,2,1,0:T(8,128)}, f32[2,38,8,1]{3,2,1,0:T(8,128)S(1)}, u32[]{:S(2)}, u32[]{:S(2)}) collective-permute-start(f32[2,38,8,1]{3,2,1,0:T(8,128)} %get-tuple-element.121), channel_id=1, source_target_pairs={{8,0},{16,8},{24,16},{32,24},{40,32},{48,40},{56,48},{64,56},{72,6... | collective-permute-start | bytes 7304 | tf_op jit(solution)/shard_map/ppermute | solution.py:29
  206.0 19.1 %collective-permute-start.25 = (f32[2,38,8,1]{3,2,1,0:T(8,128)}, f32[2,38,8,1]{3,2,1,0:T(8,128)}, u32[]{:S(2)}, u32[]{:S(2)}) collective-permute-start(f32[2,38,8,1]{3,2,1,0:T(8,128)} %get-tuple-element.122), channel_id=1, source_target_pairs={{0,8},{8,16},{16,24},{24,32},{32,40},{40,48},{48,56},{56,64},{64,7... | collective-permute-start | bytes 7304 | tf_op jit(solution)/shard_map/ppermute | solution.py:28
  220.8 10.1 %collective-permute-start.36 = (bf16[2,38,128]{2,0,1:T(2,128)(2,1)}, bf16[2,38,128]{2,0,1:T(2,128)(2,1)S(1)}, u32[]{:S(2)}, u32[]{:S(2)}) collective-permute-start(bf16[2,38,128]{2,0,1:T(2,128)(2,1)} %collective-permute-done.35), channel_id=1, source_target_pairs={{0,64},{64,0},{8,72},{72,8},{16,80},{80,16},{24,88},{88,24},{32,96... | collective-permute-start | bytes 58376 | tf_op jit(solution)/shard_map/ppermute | solution.py:18
  227.4 24.1 %collective-permute-start.32 = (f32[2,38,1,130]{3,2,1,0:T(1,128)}, f32[2,38,1,130]{3,2,1,0:T(1,128)S(1)}, u32[]{:S(2)}, u32[]{:S(2)}) collective-permute-start(f32[2,38,1,130]{3,2,1,0:T(1,128)} %get-tuple-element.108), channel_id=1, source_target_pairs={{1,0},{2,1},{3,2},{4,3},{5,4},{6,5},{7,6},{0,7},{9,8},{10,9},{11,1... | collective-permute-start | bytes 118568 | tf_op jit(solution)/shard_map/ppermute | solution.py:29
  230.9 18.1 %collective-permute-start.37 = (bf16[2,38,128]{2,0,1:T(2,128)(2,1)S(1)}, bf16[2,38,128]{2,0,1:T(2,128)(2,1)}, u32[]{:S(2)}, u32[]{:S(2)}) collective-permute-start(bf16[2,38,128]{2,0,1:T(2,128)(2,1)S(1)} %collective-permute-done.36), channel_id=1, source_target_pairs={{0,128},{128,0},{8,136},{136,8},{16,144},{144,16},{24,152},{152,24... | collective-permute-start | bytes 58376 | tf_op jit(solution)/shard_map/ppermute | solution.py:18
  239.0 19.9 %collective-permute-start.39 = (f32[2,38,1,130]{3,2,1,0:T(1,128)}, f32[2,38,1,130]{3,2,1,0:T(1,128)}, u32[]{:S(2)}, u32[]{:S(2)}) collective-permute-start(f32[2,38,1,130]{3,2,1,0:T(1,128)} %get-tuple-element.109), channel_id=1, source_target_pairs={{0,1},{1,2},{2,3},{3,4},{4,5},{5,6},{6,7},{7,0},{8,9},{9,10},{10,1... | collective-permute-start | bytes 118568 | tf_op jit(solution)/shard_map/ppermute | solution.py:28
  (40 other events, 276.8 us)
where the time goes:
time: 264 us; the launch traced here: 262 us
  starting transfers between devices  167 us (63%)
  waiting for transfers between devices  35.3 us (13%)
  other arithmetic  31.8 us (12%)
  local copies, waits for them, and re-layouts  26 us (10%)
    ppermute x24, starting transfers between devices, from_partner(): return lax.ppermute(block, axis, route)  72.1 us
    ppermute x8, starting transfers between devices, with_halo(): after = lax.ppermute(first, axis, down)  38.9 us
    ppermute x8, starting transfers between devices, with_halo(): before = lax.ppermute(last, axis, up)  36.7 us
    ppermute x24, waiting for transfers between devices, from_partner(): return lax.ppermute(block, axis, route)  20.2 us
    all_to_all x2, starting transfers between devices, shards(): lax.all_to_all(request, 'lat', split_axis=2, concat_axis=2, tiled=True)  19.3 us
    all_to_all x2, waiting for transfers between devices, shards(): lax.all_to_all(request, 'lat', split_axis=2, concat_axis=2, tiled=True)  8.44 us
    unnamed x64, local copies, waits for them, and re-layouts  7.48 us
    ppermute x8, waiting for transfers between devices, with_halo(): after = lax.ppermute(first, axis, down)  6.61 us
  transfers between devices with their start and end apart: 42, of which 10 were waited for; matrix products, arithmetic and copies ran while one was open for 18% of the time, Pallas kernels for 0%

commit v1 on v0

--- a/solution.py
+++ b/solution.py
@@ -111,7 +111,12 @@
     merid_total = jnp.zeros((levels, tile_height, tile_width), jnp.float32)
     for step_index in range(STEPS - 1, -1, -1):
         request = jnp.take(store, slot_table[step_index], axis=2)
-        received = lax.all_to_all(request, "lat", split_axis=2, concat_axis=2, tiled=True)
+        received = jnp.concatenate(
+            lax.all_to_all(
+                jnp.stack(jnp.split(request, lax.axis_size("lat"), axis=2)), "lat", 0, 0
+            ),
+            axis=2,
+        )
         order = (jnp.arange(bands, dtype=jnp.int32) + offset_steps[step_index]) % bands
         ordered = jnp.take(received, order, axis=2)
         trajectory = ordered.reshape(received.shape[0], received.shape[1], tile_height, tile_width)

time: 264 us -> 273 us (1.034)
  local copies, waits for them, and re-layouts: 26 us -> 35.9 us
    unnamed x64 -> x78, local copies, waits for them, and re-layouts: 7.48 us -> 16.3 us
  transfers between devices with their start and end apart: 42 -> 42, of which waited for: 10 -> 10; matrix products, arithmetic and copies ran while one was open for 18% -> 19% of each run, Pallas kernels for 0% -> 0%
where the time goes in v1:
time: 273 us; the launch traced here: 271 us
  starting transfers between devices  167 us (61%)
  local copies, waits for them, and re-layouts  35.9 us (13%)
  waiting for transfers between devices  35.8 us (13%)
  other arithmetic  30.8 us (11%)
    ppermute x24, starting transfers between devices, from_partner(): return lax.ppermute(block, axis, route)  71.6 us
    ppermute x8, starting transfers between devices, with_halo(): after = lax.ppermute(first, axis, down)  39 us
    ppermute x8, starting transfers between devices, with_halo(): before = lax.ppermute(last, axis, up)  36.7 us
    ppermute x24, waiting for transfers between devices, from_partner(): return lax.ppermute(block, axis, route)  20.8 us
    all_to_all x2, starting transfers between devices, shards(): lax.all_to_all(jnp.stack(jnp.split(request, lax.axis_size('lat'), axis=2)...  19.4 us
    unnamed x78, local copies, waits for them, and re-layouts  16.3 us
    all_to_all x2, waiting for transfers between devices, shards(): lax.all_to_all(jnp.stack(jnp.split(request, lax.axis_size('lat'), axis=2)...  8.39 us
    ppermute x8, waiting for transfers between devices, with_halo(): after = lax.ppermute(first, axis, down)  6.62 us
  transfers between devices with their start and end apart: 42, of which 10 were waited for; matrix products, arithmetic and copies ran while one was open for 19% of the time, Pallas kernels for 0%

profile of v1, /device:TPU:6, one launch (start us, length us, event | category | flops | bytes accessed | tf_op | source)
XLA Modules:
  0.0 270.9 jit_solution(8069381072226627563)
XLA Ops:
  9.4 10.2 %all-to-all-start.1 = ((bf16[8,4,38,1,1,128]{5,1,2,4,3,0:T(4,128)(2,1)}), bf16[8,4,38,1,1,128]{5,1,2,4,3,0:T(4,128)(2,1)S(1)}, u32[]{:S(2)}, u32[]{:S(2)}) async-start(bf16[8,4,38,1,1,128]{5,1,2,4,3,0:T(4,128)(2,1)} %fusion.54), calls=%async_computation.1 | async-start | bytes 622592 | tf_op jit(solution)/shard_map/all_to_all | solution.py:115
  20.4 10.2 %collective-permute-start = (f32[2,38,8,1]{3,2,1,0:T(8,128)S(1)}, f32[2,38,8,1]{3,2,1,0:T(8,128)S(1)}, u32[]{:S(2)}, u32[]{:S(2)}) collective-permute-start(f32[2,38,8,1]{3,2,1,0:T(8,128)S(1)} %get-tuple-element.132), channel_id=1, source_target_pairs={{8,0},{16,8},{24,16},{32,24},{40,32},{48,40},{56,48},{64,56},{72,6... | collective-permute-start | bytes 7304 | tf_op jit(solution)/shard_map/ppermute | solution.py:29
  45.1 5.1 %select_add_fusion = f32[37,8,128]{2,1,0:T(8,128)S(1)} fusion(s32[37,8,128]{2,1,0:T(8,128)S(1)} %copy-done.26, f32[]{:T(128)} %bitcast.38, f32[]{:T(128)} %bitcast.37, f32[]{:T(128)} %bitcast.36, f32[]{:T(128)} %bitcast.35, f32[]{:T(128)} %bitcast.34, f32[]{:T(128)} %bitcast.33, f32[]{:T(128)} %bitcast.32, f32[]{:T(128)} %bitcast.31), kind=kLoop, calls=%fused_computation.94 | loop fusion | flops 871424 | bytes 303136 | tf_op jit(solution)/shard_map/add | solution.py:91
  53.6 3.1 %collective-permute-done.14 = bf16[2,38,128]{2,0,1:T(2,128)(2,1)S(1)} collective-permute-done((bf16[2,38,128]{2,0,1:T(2,128)(2,1)S(1)}, bf16[2,38,128]{2,0,1:T(2,128)(2,1)S(1)}, u32[]{:S(2)}, u32[]{:S(2)}) %collective-permute-start.14) | collective-permute-done | bytes 19488 | tf_op jit(solution)/shard_map/ppermute | solution.py:18
  59.2 4.0 %collective-permute-done.15 = bf16[2,38,128]{2,0,1:T(2,128)(2,1)S(1)} collective-permute-done((bf16[2,38,128]{2,0,1:T(2,128)(2,1)S(1)}, bf16[2,38,128]{2,0,1:T(2,128)(2,1)S(1)}, u32[]{:S(2)}, u32[]{:S(2)}) %collective-permute-start.15) | collective-permute-done | bytes 19488 | tf_op jit(solution)/shard_map/ppermute | solution.py:18
  63.3 4.7 %collective-permute-start.16 = (bf16[2,38,128]{2,0,1:T(2,128)(2,1)S(1)}, bf16[2,38,128]{2,0,1:T(2,128)(2,1)S(1)}, u32[]{:S(2)}, u32[]{:S(2)}) collective-permute-start(bf16[2,38,128]{2,0,1:T(2,128)(2,1)S(1)} %collective-permute-done.15), channel_id=1, source_target_pairs={{0,64},{64,0},{8,72},{72,8},{16,80},{80,16},{24,88},{88,24},{32,96... | collective-permute-start | bytes 58376 | tf_op jit(solution)/shard_map/ppermute | solution.py:18
  68.5 2.8 %collective-permute-start.12 = (f32[2,38,1,130]{3,2,1,0:T(1,128)S(1)}, f32[2,38,1,130]{3,2,1,0:T(1,128)S(1)}, u32[]{:S(2)}, u32[]{:S(2)}) collective-permute-start(f32[2,38,1,130]{3,2,1,0:T(1,128)S(1)} %get-tuple-element.112), channel_id=1, source_target_pairs={{1,0},{2,1},{3,2},{4,3},{5,4},{6,5},{7,6},{0,7},{9,8},{10,9},{11,1... | collective-permute-start | bytes 118568 | tf_op jit(solution)/shard_map/ppermute | solution.py:29
  72.8 3.0 %collective-permute-start.17 = (bf16[2,38,128]{2,0,1:T(2,128)(2,1)S(1)}, bf16[2,38,128]{2,0,1:T(2,128)(2,1)S(1)}, u32[]{:S(2)}, u32[]{:S(2)}) collective-permute-start(bf16[2,38,128]{2,0,1:T(2,128)(2,1)S(1)} %collective-permute-done.16), channel_id=1, source_target_pairs={{0,128},{128,0},{8,136},{136,8},{16,144},{144,16},{24,152},{152,24... | collective-permute-start | bytes 58376 | tf_op jit(solution)/shard_map/ppermute | solution.py:18
  75.9 7.3 %collective-permute-start.19 = (f32[2,38,1,130]{3,2,1,0:T(1,128)S(1)}, f32[2,38,1,130]{3,2,1,0:T(1,128)}, u32[]{:S(2)}, u32[]{:S(2)}) collective-permute-start(f32[2,38,1,130]{3,2,1,0:T(1,128)S(1)} %get-tuple-element.113), channel_id=1, source_target_pairs={{0,1},{1,2},{2,3},{3,4},{4,5},{5,6},{6,7},{7,0},{8,9},{9,10},{10,1... | collective-permute-start | bytes 118568 | tf_op jit(solution)/shard_map/ppermute | solution.py:28
  83.2 4.4 %collective-permute-start.18 = (bf16[2,38,128]{2,0,1:T(2,128)(2,1)S(1)}, bf16[2,38,128]{2,0,1:T(2,128)(2,1)S(1)}, u32[]{:S(2)}, u32[]{:S(2)}) collective-permute-start(bf16[2,38,128]{2,0,1:T(2,128)(2,1)S(1)} %collective-permute-done.17), channel_id=1, source_target_pairs={{0,256},{256,0},{8,264},{264,8},{16,272},{272,16},{24,280},{280,24... | collective-permute-start | bytes 58376 | tf_op jit(solution)/shard_map/ppermute | solution.py:18
  90.9 9.2 %all-to-all-start = ((bf16[8,4,38,1,1,128]{5,1,2,4,3,0:T(4,128)(2,1)}), bf16[8,4,38,1,1,128]{5,1,2,4,3,0:T(4,128)(2,1)S(1)}, u32[]{:S(2)}, u32[]{:S(2)}) async-start(bf16[8,4,38,1,1,128]{5,1,2,4,3,0:T(4,128)(2,1)} %fusion.62), calls=%async_computation | async-start | bytes 622592 | tf_op jit(solution)/shard_map/all_to_all | solution.py:115
  102.1 8.4 %all-to-all-done = bf16[8,4,38,1,1,128]{5,1,2,4,3,0:T(4,128)(2,1)S(1)} async-done(((bf16[8,4,38,1,1,128]{5,1,2,4,3,0:T(4,128)(2,1)}), bf16[8,4,38,1,1,128]{5,1,2,4,3,0:T(4,128)(2,1)S(1)}, u32[]{:S(2)}, u32[]{:S(2)}) %all-to-all-start) | async-done | bytes 311328 | tf_op jit(solution)/shard_map/all_to_all | solution.py:115
  114.0 7.5 %collective-permute-start.22 = (bf16[4,38,8,1]{3,2,1,0:T(8,128)(2,1)S(1)}, bf16[4,38,8,1]{3,2,1,0:T(8,128)(2,1)S(1)}, u32[]{:S(2)}, u32[]{:S(2)}) collective-permute-start(bf16[4,38,8,1]{3,2,1,0:T(8,128)(2,1)S(1)} %get-tuple-element.120), channel_id=1, source_target_pairs={{8,0},{16,8},{24,16},{32,24},{40,32},{48,40},{56,48},{64,56},{72,6... | collective-permute-start | bytes 7304 | tf_op jit(solution)/shard_map/ppermute | solution.py:29
  123.5 7.5 %collective-permute-start.2 = (bf16[4,38,8,1]{3,2,1,0:T(8,128)(2,1)S(1)}, bf16[4,38,8,1]{3,2,1,0:T(8,128)(2,1)S(1)}, u32[]{:S(2)}, u32[]{:S(2)}) collective-permute-start(bf16[4,38,8,1]{3,2,1,0:T(8,128)(2,1)S(1)} %get-tuple-element.131), channel_id=1, source_target_pairs={{8,0},{16,8},{24,16},{32,24},{40,32},{48,40},{56,48},{64,56},{72,6... | collective-permute-start | bytes 7304 | tf_op jit(solution)/shard_map/ppermute | solution.py:29
  134.6 2.4 collective-permute-start.6
  137.8 2.9 %collective-permute-start.23 = (bf16[4,38,1,130]{3,2,1,0:T(2,128)(2,1)S(1)}, bf16[4,38,1,130]{3,2,1,0:T(2,128)(2,1)S(1)}, u32[]{:S(2)}, u32[]{:S(2)}) collective-permute-start(bf16[4,38,1,130]{3,2,1,0:T(2,128)(2,1)S(1)} %get-tuple-element.106), channel_id=1, source_target_pairs={{0,1},{1,2},{2,3},{3,4},{4,5},{5,6},{6,7},{7,0},{8,9},{9,10},{10,1... | collective-permute-start | bytes 118568 | tf_op jit(solution)/shard_map/ppermute | solution.py:28
  140.7 2.9 %collective-permute-start.24 = (bf16[4,38,1,130]{3,2,1,0:T(2,128)(2,1)S(1)}, bf16[4,38,1,130]{3,2,1,0:T(2,128)(2,1)S(1)}, u32[]{:S(2)}, u32[]{:S(2)}) collective-permute-start(bf16[4,38,1,130]{3,2,1,0:T(2,128)(2,1)S(1)} %get-tuple-element.107), channel_id=1, source_target_pairs={{1,0},{2,1},{3,2},{4,3},{5,4},{6,5},{7,6},{0,7},{9,8},{10,9},{11,1... | collective-permute-start | bytes 118568 | tf_op jit(solution)/shard_map/ppermute | solution.py:29
  144.4 8.9 %collective-permute-start.3 = (bf16[4,38,1,130]{3,2,1,0:T(2,128)(2,1)S(1)}, bf16[4,38,1,130]{3,2,1,0:T(2,128)(2,1)S(1)}, u32[]{:S(2)}, u32[]{:S(2)}) collective-permute-start(bf16[4,38,1,130]{3,2,1,0:T(2,128)(2,1)S(1)} %get-tuple-element.110), channel_id=1, source_target_pairs={{0,1},{1,2},{2,3},{3,4},{4,5},{5,6},{6,7},{7,0},{8,9},{9,10},{10,1... | collective-permute-start | bytes 118568 | tf_op jit(solution)/shard_map/ppermute | solution.py:28
  157.3 3.9 %collective-permute-start.7 = (bf16[3,38,128]{2,0,1:T(4,128)(2,1)S(1)}, bf16[3,38,128]{2,0,1:T(4,128)(2,1)S(1)}, u32[]{:S(2)}, u32[]{:S(2)}) collective-permute-start(bf16[3,38,128]{2,0,1:T(4,128)(2,1)S(1)} %collective-permute-done.6), channel_id=1, source_target_pairs={{0,16},{16,0},{8,24},{24,8},{32,48},{48,32},{40,56},{56,40},{64,80... | collective-permute-start | bytes 87560 | tf_op jit(solution)/shard_map/ppermute | solution.py:18
  162.3 6.6 %collective-permute-done.4 = bf16[4,38,1,130]{3,2,1,0:T(2,128)(2,1)S(1)} collective-permute-done((bf16[4,38,1,130]{3,2,1,0:T(2,128)(2,1)S(1)}, bf16[4,38,1,130]{3,2,1,0:T(2,128)(2,1)S(1)}, u32[]{:S(2)}, u32[]{:S(2)}) %collective-permute-start.4) | collective-permute-done | bytes 39552 | tf_op jit(solution)/shard_map/ppermute | solution.py:29
  173.6 4.8 %collective-permute-start.28 = (bf16[3,38,128]{2,0,1:T(4,128)(2,1)S(1)}, bf16[3,38,128]{2,0,1:T(4,128)(2,1)S(1)}, u32[]{:S(2)}, u32[]{:S(2)}) collective-permute-start(bf16[3,38,128]{2,0,1:T(4,128)(2,1)S(1)} %collective-permute-done.27), channel_id=1, source_target_pairs={{0,32},{32,0},{8,40},{40,8},{16,48},{48,16},{24,56},{56,24},{64,96... | collective-permute-start | bytes 87560 | tf_op jit(solution)/shard_map/ppermute | solution.py:18
  181.1 7.8 %collective-permute-start.29 = (bf16[3,38,128]{2,0,1:T(4,128)(2,1)S(1)}, bf16[3,38,128]{2,0,1:T(4,128)(2,1)S(1)}, u32[]{:S(2)}, u32[]{:S(2)}) collective-permute-start(bf16[3,38,128]{2,0,1:T(4,128)(2,1)S(1)} %collective-permute-done.28), channel_id=1, source_target_pairs={{0,64},{64,0},{8,72},{72,8},{16,80},{80,16},{24,88},{88,24},{32,96... | collective-permute-start | bytes 87560 | tf_op jit(solution)/shard_map/ppermute | solution.py:18
  191.1 3.9 %collective-permute-start.30 = (bf16[3,38,128]{2,0,1:T(4,128)(2,1)S(1)}, bf16[3,38,128]{2,0,1:T(4,128)(2,1)}, u32[]{:S(2)}, u32[]{:S(2)}) collective-permute-start(bf16[3,38,128]{2,0,1:T(4,128)(2,1)S(1)} %collective-permute-done.29), channel_id=1, source_target_pairs={{0,128},{128,0},{8,136},{136,8},{16,144},{144,16},{24,152},{152,24... | collective-permute-start | bytes 87560 | tf_op jit(solution)/shard_map/ppermute | solution.py:18
  197.9 4.8 %collective-permute-start.31 = (bf16[3,38,128]{2,0,1:T(4,128)(2,1)}, bf16[3,38,128]{2,0,1:T(4,128)(2,1)}, u32[]{:S(2)}, u32[]{:S(2)}) collective-permute-start(bf16[3,38,128]{2,0,1:T(4,128)(2,1)} %collective-permute-done.30), channel_id=1, source_target_pairs={{0,256},{256,0},{8,264},{264,8},{16,272},{272,16},{24,280},{280,24... | collective-permute-start | bytes 87560 | tf_op jit(solution)/shard_map/ppermute | solution.py:18
  211.1 4.0 %collective-permute-start.20 = (f32[2,38,8,1]{3,2,1,0:T(8,128)}, f32[2,38,8,1]{3,2,1,0:T(8,128)S(1)}, u32[]{:S(2)}, u32[]{:S(2)}) collective-permute-start(f32[2,38,8,1]{3,2,1,0:T(8,128)} %get-tuple-element.121), channel_id=1, source_target_pairs={{8,0},{16,8},{24,16},{32,24},{40,32},{48,40},{56,48},{64,56},{72,6... | collective-permute-start | bytes 7304 | tf_op jit(solution)/shard_map/ppermute | solution.py:29
  219.7 3.4 %collective-permute-done.34 = bf16[2,38,128]{2,0,1:T(2,128)(2,1)} collective-permute-done((bf16[2,38,128]{2,0,1:T(2,128)(2,1)}, bf16[2,38,128]{2,0,1:T(2,128)(2,1)}, u32[]{:S(2)}, u32[]{:S(2)}) %collective-permute-start.34) | collective-permute-done | bytes 19488 | tf_op jit(solution)/shard_map/ppermute | solution.py:18
  229.9 4.2 %collective-permute-start.36 = (bf16[2,38,128]{2,0,1:T(2,128)(2,1)}, bf16[2,38,128]{2,0,1:T(2,128)(2,1)S(1)}, u32[]{:S(2)}, u32[]{:S(2)}) collective-permute-start(bf16[2,38,128]{2,0,1:T(2,128)(2,1)} %collective-permute-done.35), channel_id=1, source_target_pairs={{0,64},{64,0},{8,72},{72,8},{16,80},{80,16},{24,88},{88,24},{32,96... | collective-permute-start | bytes 58376 | tf_op jit(solution)/shard_map/ppermute | solution.py:18
  234.2 2.3 pad_maximum_fusion.25
  239.9 2.5 collective-permute-start.37
  248.1 9.9 %collective-permute-start.39 = (f32[2,38,1,130]{3,2,1,0:T(1,128)}, f32[2,38,1,130]{3,2,1,0:T(1,128)}, u32[]{:S(2)}, u32[]{:S(2)}) collective-permute-start(f32[2,38,1,130]{3,2,1,0:T(1,128)} %get-tuple-element.109), channel_id=1, source_target_pairs={{0,1},{1,2},{2,3},{3,4},{4,5},{5,6},{6,7},{7,0},{8,9},{9,10},{10,1... | collective-permute-start | bytes 118568 | tf_op jit(solution)/shard_map/ppermute | solution.py:28
  261.5 3.4 %collective-permute-done.38 = bf16[2,38,128]{2,0,1:T(2,128)(2,1)S(1)} collective-permute-done((bf16[2,38,128]{2,0,1:T(2,128)(2,1)}, bf16[2,38,128]{2,0,1:T(2,128)(2,1)S(1)}, u32[]{:S(2)}, u32[]{:S(2)}) %collective-permute-start.38) | collective-permute-done | bytes 19488 | tf_op jit(solution)/shard_map/ppermute | solution.py:18
  268.6 2.3 fusion.15
  (223 shorter events, 100.8 us)
Async XLA Ops:
  9.4 80.8 %all-to-all-start.1 = ((bf16[8,4,38,1,1,128]{5,1,2,4,3,0:T(4,128)(2,1)}), bf16[8,4,38,1,1,128]{5,1,2,4,3,0:T(4,128)(2,1)S(1)}, u32[]{:S(2)}, u32[]{:S(2)}) async-start(bf16[8,4,38,1,1,128]{5,1,2,4,3,0:T(4,128)(2,1)} %fusion.54), calls=%async_computation.1 | async-start | bytes 622592 | tf_op jit(solution)/shard_map/all_to_all | solution.py:115
  20.4 47.5 %collective-permute-start = (f32[2,38,8,1]{3,2,1,0:T(8,128)S(1)}, f32[2,38,8,1]{3,2,1,0:T(8,128)S(1)}, u32[]{:S(2)}, u32[]{:S(2)}) collective-permute-start(f32[2,38,8,1]{3,2,1,0:T(8,128)S(1)} %get-tuple-element.132), channel_id=1, source_target_pairs={{8,0},{16,8},{24,16},{32,24},{40,32},{48,40},{56,48},{64,56},{72,6... | collective-permute-start | bytes 7304 | tf_op jit(solution)/shard_map/ppermute | solution.py:29
  30.6 37.4 %collective-permute-start.5 = (f32[2,38,8,1]{3,2,1,0:T(8,128)S(1)}, f32[2,38,8,1]{3,2,1,0:T(8,128)S(1)}, u32[]{:S(2)}, u32[]{:S(2)}) collective-permute-start(f32[2,38,8,1]{3,2,1,0:T(8,128)S(1)} %get-tuple-element.133), channel_id=1, source_target_pairs={{0,8},{8,16},{16,24},{24,32},{32,40},{40,48},{48,56},{56,64},{64,7... | collective-permute-start | bytes 7304 | tf_op jit(solution)/shard_map/ppermute | solution.py:28
  32.6 18.4 %collective-permute-start.13 = (bf16[2,38,128]{2,0,1:T(2,128)(2,1)S(1)}, bf16[2,38,128]{2,0,1:T(2,128)(2,1)S(1)}, u32[]{:S(2)}, u32[]{:S(2)}) collective-permute-start(bf16[2,38,128]{2,0,1:T(2,128)(2,1)S(1)} %bitcast.215), channel_id=1, source_target_pairs={{0,8},{8,0},{16,24},{24,16},{32,40},{40,32},{48,56},{56,48},{64,72... | collective-permute-start | bytes 58376 | tf_op jit(solution)/shard_map/ppermute | solution.py:18
  63.3 9.6 %collective-permute-start.16 = (bf16[2,38,128]{2,0,1:T(2,128)(2,1)S(1)}, bf16[2,38,128]{2,0,1:T(2,128)(2,1)S(1)}, u32[]{:S(2)}, u32[]{:S(2)}) collective-permute-start(bf16[2,38,128]{2,0,1:T(2,128)(2,1)S(1)} %collective-permute-done.15), channel_id=1, source_target_pairs={{0,64},{64,0},{8,72},{72,8},{16,80},{80,16},{24,88},{88,24},{32,96... | collective-permute-start | bytes 58376 | tf_op jit(solution)/shard_map/ppermute | solution.py:18
  68.5 19.0 %collective-permute-start.12 = (f32[2,38,1,130]{3,2,1,0:T(1,128)S(1)}, f32[2,38,1,130]{3,2,1,0:T(1,128)S(1)}, u32[]{:S(2)}, u32[]{:S(2)}) collective-permute-start(f32[2,38,1,130]{3,2,1,0:T(1,128)S(1)} %get-tuple-element.112), channel_id=1, source_target_pairs={{1,0},{2,1},{3,2},{4,3},{5,4},{6,5},{7,6},{0,7},{9,8},{10,9},{11,1... | collective-permute-start | bytes 118568 | tf_op jit(solution)/shard_map/ppermute | solution.py:29
  72.8 10.3 %collective-permute-start.17 = (bf16[2,38,128]{2,0,1:T(2,128)(2,1)S(1)}, bf16[2,38,128]{2,0,1:T(2,128)(2,1)S(1)}, u32[]{:S(2)}, u32[]{:S(2)}) collective-permute-start(bf16[2,38,128]{2,0,1:T(2,128)(2,1)S(1)} %collective-permute-done.16), channel_id=1, source_target_pairs={{0,128},{128,0},{8,136},{136,8},{16,144},{144,16},{24,152},{152,24... | collective-permute-start | bytes 58376 | tf_op jit(solution)/shard_map/ppermute | solution.py:18
  75.9 127.2 %collective-permute-start.19 = (f32[2,38,1,130]{3,2,1,0:T(1,128)S(1)}, f32[2,38,1,130]{3,2,1,0:T(1,128)}, u32[]{:S(2)}, u32[]{:S(2)}) collective-permute-start(f32[2,38,1,130]{3,2,1,0:T(1,128)S(1)} %get-tuple-element.113), channel_id=1, source_target_pairs={{0,1},{1,2},{2,3},{3,4},{4,5},{5,6},{6,7},{7,0},{8,9},{9,10},{10,1... | collective-permute-start | bytes 118568 | tf_op jit(solution)/shard_map/ppermute | solution.py:28
  90.9 19.6 %all-to-all-start = ((bf16[8,4,38,1,1,128]{5,1,2,4,3,0:T(4,128)(2,1)}), bf16[8,4,38,1,1,128]{5,1,2,4,3,0:T(4,128)(2,1)S(1)}, u32[]{:S(2)}, u32[]{:S(2)}) async-start(bf16[8,4,38,1,1,128]{5,1,2,4,3,0:T(4,128)(2,1)} %fusion.62), calls=%async_computation | async-start | bytes 622592 | tf_op jit(solution)/shard_map/all_to_all | solution.py:115
  112.1 20.6 %collective-permute-start.21 = (bf16[4,38,8,1]{3,2,1,0:T(8,128)(2,1)}, bf16[4,38,8,1]{3,2,1,0:T(8,128)(2,1)S(1)}, u32[]{:S(2)}, u32[]{:S(2)}) collective-permute-start(bf16[4,38,8,1]{3,2,1,0:T(8,128)(2,1)} %get-tuple-element.119), channel_id=1, source_target_pairs={{0,8},{8,16},{16,24},{24,32},{32,40},{40,48},{48,56},{56,64},{64,7... | collective-permute-start | bytes 7304 | tf_op jit(solution)/shard_map/ppermute | solution.py:28
  114.0 20.6 %collective-permute-start.22 = (bf16[4,38,8,1]{3,2,1,0:T(8,128)(2,1)S(1)}, bf16[4,38,8,1]{3,2,1,0:T(8,128)(2,1)S(1)}, u32[]{:S(2)}, u32[]{:S(2)}) collective-permute-start(bf16[4,38,8,1]{3,2,1,0:T(8,128)(2,1)S(1)} %get-tuple-element.120), channel_id=1, source_target_pairs={{8,0},{16,8},{24,16},{32,24},{40,32},{48,40},{56,48},{64,56},{72,6... | collective-permute-start | bytes 7304 | tf_op jit(solution)/shard_map/ppermute | solution.py:29
  121.5 16.2 %collective-permute-start.1 = (bf16[4,38,8,1]{3,2,1,0:T(8,128)(2,1)S(1)}, bf16[4,38,8,1]{3,2,1,0:T(8,128)(2,1)S(1)}, u32[]{:S(2)}, u32[]{:S(2)}) collective-permute-start(bf16[4,38,8,1]{3,2,1,0:T(8,128)(2,1)S(1)} %get-tuple-element.130), channel_id=1, source_target_pairs={{0,8},{8,16},{16,24},{24,32},{32,40},{40,48},{48,56},{56,64},{64,7... | collective-permute-start | bytes 7304 | tf_op jit(solution)/shard_map/ppermute | solution.py:28
  123.5 17.2 %collective-permute-start.2 = (bf16[4,38,8,1]{3,2,1,0:T(8,128)(2,1)S(1)}, bf16[4,38,8,1]{3,2,1,0:T(8,128)(2,1)S(1)}, u32[]{:S(2)}, u32[]{:S(2)}) collective-permute-start(bf16[4,38,8,1]{3,2,1,0:T(8,128)(2,1)S(1)} %get-tuple-element.131), channel_id=1, source_target_pairs={{8,0},{16,8},{24,16},{32,24},{40,32},{48,40},{56,48},{64,56},{72,6... | collective-permute-start | bytes 7304 | tf_op jit(solution)/shard_map/ppermute | solution.py:29
  132.6 11.8 %collective-permute-start.26 = (bf16[3,38,128]{2,0,1:T(4,128)(2,1)S(1)}, bf16[3,38,128]{2,0,1:T(4,128)(2,1)S(1)}, u32[]{:S(2)}, u32[]{:S(2)}) collective-permute-start(bf16[3,38,128]{2,0,1:T(4,128)(2,1)S(1)} %pad_maximum_fusion.38), channel_id=1, source_target_pairs={{0,8},{8,0},{16,24},{24,16},{32,40},{40,32},{48,56},{56,48},{64,72... | collective-permute-start | bytes 87560 | tf_op jit(solution)/shard_map/ppermute | solution.py:18
  134.6 18.8 %collective-permute-start.6 = (bf16[3,38,128]{2,0,1:T(4,128)(2,1)S(1)}, bf16[3,38,128]{2,0,1:T(4,128)(2,1)S(1)}, u32[]{:S(2)}, u32[]{:S(2)}) collective-permute-start(bf16[3,38,128]{2,0,1:T(4,128)(2,1)S(1)} %pad_maximum_fusion.37), channel_id=1, source_target_pairs={{0,8},{8,0},{16,24},{24,16},{32,40},{40,32},{48,56},{56,48},{64,72... | collective-permute-start | bytes 87560 | tf_op jit(solution)/shard_map/ppermute | solution.py:18
  137.8 17.5 %collective-permute-start.23 = (bf16[4,38,1,130]{3,2,1,0:T(2,128)(2,1)S(1)}, bf16[4,38,1,130]{3,2,1,0:T(2,128)(2,1)S(1)}, u32[]{:S(2)}, u32[]{:S(2)}) collective-permute-start(bf16[4,38,1,130]{3,2,1,0:T(2,128)(2,1)S(1)} %get-tuple-element.106), channel_id=1, source_target_pairs={{0,1},{1,2},{2,3},{3,4},{4,5},{5,6},{6,7},{7,0},{8,9},{9,10},{10,1... | collective-permute-start | bytes 118568 | tf_op jit(solution)/shard_map/ppermute | solution.py:28
  140.7 16.5 %collective-permute-start.24 = (bf16[4,38,1,130]{3,2,1,0:T(2,128)(2,1)S(1)}, bf16[4,38,1,130]{3,2,1,0:T(2,128)(2,1)S(1)}, u32[]{:S(2)}, u32[]{:S(2)}) collective-permute-start(bf16[4,38,1,130]{3,2,1,0:T(2,128)(2,1)S(1)} %get-tuple-element.107), channel_id=1, source_target_pairs={{1,0},{2,1},{3,2},{4,3},{5,4},{6,5},{7,6},{0,7},{9,8},{10,9},{11,1... | collective-permute-start | bytes 118568 | tf_op jit(solution)/shard_map/ppermute | solution.py:29
  144.4 17.9 %collective-permute-start.3 = (bf16[4,38,1,130]{3,2,1,0:T(2,128)(2,1)S(1)}, bf16[4,38,1,130]{3,2,1,0:T(2,128)(2,1)S(1)}, u32[]{:S(2)}, u32[]{:S(2)}) collective-permute-start(bf16[4,38,1,130]{3,2,1,0:T(2,128)(2,1)S(1)} %get-tuple-element.110), channel_id=1, source_target_pairs={{0,1},{1,2},{2,3},{3,4},{4,5},{5,6},{6,7},{7,0},{8,9},{9,10},{10,1... | collective-permute-start | bytes 118568 | tf_op jit(solution)/shard_map/ppermute | solution.py:28
  153.4 15.5 %collective-permute-start.4 = (bf16[4,38,1,130]{3,2,1,0:T(2,128)(2,1)S(1)}, bf16[4,38,1,130]{3,2,1,0:T(2,128)(2,1)S(1)}, u32[]{:S(2)}, u32[]{:S(2)}) collective-permute-start(bf16[4,38,1,130]{3,2,1,0:T(2,128)(2,1)S(1)} %get-tuple-element.111), channel_id=1, source_target_pairs={{1,0},{2,1},{3,2},{4,3},{5,4},{6,5},{7,6},{0,7},{9,8},{10,9},{11,1... | collective-permute-start | bytes 118568 | tf_op jit(solution)/shard_map/ppermute | solution.py:29
  155.3 18.3 %collective-permute-start.27 = (bf16[3,38,128]{2,0,1:T(4,128)(2,1)S(1)}, bf16[3,38,128]{2,0,1:T(4,128)(2,1)S(1)}, u32[]{:S(2)}, u32[]{:S(2)}) collective-permute-start(bf16[3,38,128]{2,0,1:T(4,128)(2,1)S(1)} %collective-permute-done.26), channel_id=1, source_target_pairs={{0,16},{16,0},{8,24},{24,8},{32,48},{48,32},{40,56},{56,40},{64,80... | collective-permute-start | bytes 87560 | tf_op jit(solution)/shard_map/ppermute | solution.py:18
  157.3 13.7 %collective-permute-start.7 = (bf16[3,38,128]{2,0,1:T(4,128)(2,1)S(1)}, bf16[3,38,128]{2,0,1:T(4,128)(2,1)S(1)}, u32[]{:S(2)}, u32[]{:S(2)}) collective-permute-start(bf16[3,38,128]{2,0,1:T(4,128)(2,1)S(1)} %collective-permute-done.6), channel_id=1, source_target_pairs={{0,16},{16,0},{8,24},{24,8},{32,48},{48,32},{40,56},{56,40},{64,80... | collective-permute-start | bytes 87560 | tf_op jit(solution)/shard_map/ppermute | solution.py:18
  178.4 10.5 %collective-permute-start.9 = (bf16[3,38,128]{2,0,1:T(4,128)(2,1)S(1)}, bf16[3,38,128]{2,0,1:T(4,128)(2,1)S(1)}, u32[]{:S(2)}, u32[]{:S(2)}) collective-permute-start(bf16[3,38,128]{2,0,1:T(4,128)(2,1)S(1)} %collective-permute-done.8), channel_id=1, source_target_pairs={{0,64},{64,0},{8,72},{72,8},{16,80},{80,16},{24,88},{88,24},{32,96... | collective-permute-start | bytes 87560 | tf_op jit(solution)/shard_map/ppermute | solution.py:18
  181.1 9.9 %collective-permute-start.29 = (bf16[3,38,128]{2,0,1:T(4,128)(2,1)S(1)}, bf16[3,38,128]{2,0,1:T(4,128)(2,1)S(1)}, u32[]{:S(2)}, u32[]{:S(2)}) collective-permute-start(bf16[3,38,128]{2,0,1:T(4,128)(2,1)S(1)} %collective-permute-done.28), channel_id=1, source_target_pairs={{0,64},{64,0},{8,72},{72,8},{16,80},{80,16},{24,88},{88,24},{32,96... | collective-permute-start | bytes 87560 | tf_op jit(solution)/shard_map/ppermute | solution.py:18
  195.0 7.7 %collective-permute-start.11 = (bf16[3,38,128]{2,0,1:T(4,128)(2,1)S(1)}, bf16[3,38,128]{2,0,1:T(4,128)(2,1)S(1)}, u32[]{:S(2)}, u32[]{:S(2)}) collective-permute-start(bf16[3,38,128]{2,0,1:T(4,128)(2,1)S(1)} %collective-permute-done.10), channel_id=1, source_target_pairs={{0,256},{256,0},{8,264},{264,8},{16,272},{272,16},{24,280},{280,24... | collective-permute-start | bytes 87560 | tf_op jit(solution)/shard_map/ppermute | solution.py:18
  197.9 12.2 %collective-permute-start.31 = (bf16[3,38,128]{2,0,1:T(4,128)(2,1)}, bf16[3,38,128]{2,0,1:T(4,128)(2,1)}, u32[]{:S(2)}, u32[]{:S(2)}) collective-permute-start(bf16[3,38,128]{2,0,1:T(4,128)(2,1)} %collective-permute-done.30), channel_id=1, source_target_pairs={{0,256},{256,0},{8,264},{264,8},{16,272},{272,16},{24,280},{280,24... | collective-permute-start | bytes 87560 | tf_op jit(solution)/shard_map/ppermute | solution.py:18
  207.4 9.7 %collective-permute-start.33 = (bf16[2,38,128]{2,0,1:T(2,128)(2,1)}, bf16[2,38,128]{2,0,1:T(2,128)(2,1)}, u32[]{:S(2)}, u32[]{:S(2)}) collective-permute-start(bf16[2,38,128]{2,0,1:T(2,128)(2,1)} %bitcast.210), channel_id=1, source_target_pairs={{0,8},{8,0},{16,24},{24,16},{32,40},{40,32},{48,56},{56,48},{64,72... | collective-permute-start | bytes 58376 | tf_op jit(solution)/shard_map/ppermute | solution.py:18
  211.1 23.0 %collective-permute-start.20 = (f32[2,38,8,1]{3,2,1,0:T(8,128)}, f32[2,38,8,1]{3,2,1,0:T(8,128)S(1)}, u32[]{:S(2)}, u32[]{:S(2)}) collective-permute-start(f32[2,38,8,1]{3,2,1,0:T(8,128)} %get-tuple-element.121), channel_id=1, source_target_pairs={{8,0},{16,8},{24,16},{32,24},{40,32},{48,40},{56,48},{64,56},{72,6... | collective-permute-start | bytes 7304 | tf_op jit(solution)/shard_map/ppermute | solution.py:29
  215.1 19.0 %collective-permute-start.25 = (f32[2,38,8,1]{3,2,1,0:T(8,128)}, f32[2,38,8,1]{3,2,1,0:T(8,128)}, u32[]{:S(2)}, u32[]{:S(2)}) collective-permute-start(f32[2,38,8,1]{3,2,1,0:T(8,128)} %get-tuple-element.122), channel_id=1, source_target_pairs={{0,8},{8,16},{16,24},{24,32},{32,40},{40,48},{48,56},{56,64},{64,7... | collective-permute-start | bytes 7304 | tf_op jit(solution)/shard_map/ppermute | solution.py:28
  229.9 10.0 %collective-permute-start.36 = (bf16[2,38,128]{2,0,1:T(2,128)(2,1)}, bf16[2,38,128]{2,0,1:T(2,128)(2,1)S(1)}, u32[]{:S(2)}, u32[]{:S(2)}) collective-permute-start(bf16[2,38,128]{2,0,1:T(2,128)(2,1)} %collective-permute-done.35), channel_id=1, source_target_pairs={{0,64},{64,0},{8,72},{72,8},{16,80},{80,16},{24,88},{88,24},{32,96... | collective-permute-start | bytes 58376 | tf_op jit(solution)/shard_map/ppermute | solution.py:18
  236.4 23.6 %collective-permute-start.32 = (f32[2,38,1,130]{3,2,1,0:T(1,128)}, f32[2,38,1,130]{3,2,1,0:T(1,128)S(1)}, u32[]{:S(2)}, u32[]{:S(2)}) collective-permute-start(f32[2,38,1,130]{3,2,1,0:T(1,128)} %get-tuple-element.108), channel_id=1, source_target_pairs={{1,0},{2,1},{3,2},{4,3},{5,4},{6,5},{7,6},{0,7},{9,8},{10,9},{11,1... | collective-permute-start | bytes 118568 | tf_op jit(solution)/shard_map/ppermute | solution.py:29
  239.9 18.1 %collective-permute-start.37 = (bf16[2,38,128]{2,0,1:T(2,128)(2,1)S(1)}, bf16[2,38,128]{2,0,1:T(2,128)(2,1)}, u32[]{:S(2)}, u32[]{:S(2)}) collective-permute-start(bf16[2,38,128]{2,0,1:T(2,128)(2,1)S(1)} %collective-permute-done.36), channel_id=1, source_target_pairs={{0,128},{128,0},{8,136},{136,8},{16,144},{144,16},{24,152},{152,24... | collective-permute-start | bytes 58376 | tf_op jit(solution)/shard_map/ppermute | solution.py:18
  248.1 19.9 %collective-permute-start.39 = (f32[2,38,1,130]{3,2,1,0:T(1,128)}, f32[2,38,1,130]{3,2,1,0:T(1,128)}, u32[]{:S(2)}, u32[]{:S(2)}) collective-permute-start(f32[2,38,1,130]{3,2,1,0:T(1,128)} %get-tuple-element.109), channel_id=1, source_target_pairs={{0,1},{1,2},{2,3},{3,4},{4,5},{5,6},{6,7},{7,0},{8,9},{9,10},{10,1... | collective-permute-start | bytes 118568 | tf_op jit(solution)/shard_map/ppermute | solution.py:28
  (40 other events, 278.6 us)
